TPU v7x, 32 devices: a whole 2x2x4 slice. The times are simulated.
32 devices in a mesh: occ: 8 (over y, x, core), ao: 4 (over z).
Axes of the slice: x: 2, y: 2, z: 4, core: 2. Of those that a mesh axis runs over, the one named last changes fastest.
Arguments:
- coef: bfloat16 [2048, 8], P('ao', 'occ'), may hold values from -0.5 to 0.5
- half_ints: bfloat16 [8, 1024, 2048], P('occ', None, 'ao'), may hold values from -0.5 to 0.5
- metric_inv: bfloat16 [64, 128, 128], replicated, may hold values from -1 to 2, as said below
- dom_blocks: int32 [8, 8], P('occ'), may hold values from 0 to 63, as said below
- dom_len: int32 [8], P('occ'), may hold values from 2 to 8
Outputs:
- exchange_k: float32 [2048, 2048], P('ao', 'occ')
- fit_density: float32 [8192], replicated
Inputs may be any that keep to these rules, and one draw needn't show every extreme that they name: `dom_blocks`: each row holds 8 different block numbers. `metric_inv`: full rank blocks.
All inputs are finite; a program needn't handle non-finite values.
Results may differ from a plain program's by a relative error of at most 0.0055.
Values may be sent and summed in bfloat16 or wider, within the bound.
No kernel may reach another device: no remote copies, remote signals or barrier semaphores. Data moves between devices by JAX's collectives and lax.ppermute only.
A program may use at most 128 MiB of HBM per device.

v0:
```python
import jax
import jax.numpy as jnp
from jax import lax
from jax.sharding import PartitionSpec as P


def on_device(coef, half_ints, metric_inv, dom_blocks, dom_len):
    lmo_count, domain, ao_rows = half_ints.shape
    block = metric_inv.shape[1]
    slots = domain // block
    fit_blocks = metric_inv.shape[0]
    metric_rows = metric_inv[dom_blocks]
    raw_ints = half_ints.reshape(lmo_count, slots, block, ao_rows)
    fitted = jnp.einsum(
        "isab,isbm->isam", metric_rows, raw_ints, preferred_element_type=jnp.float32
    )
    live_slots = jnp.arange(slots, dtype=jnp.int32)[None, :] < dom_len[:, None]
    fitted = jnp.where(live_slots[:, :, None, None], fitted, 0.0)
    fitted = fitted.reshape(lmo_count, domain, ao_rows).astype(jnp.bfloat16)
    pair_part = jnp.einsum("ipm,mi->ip", fitted, coef, preferred_element_type=jnp.float32)
    one_hot = (
        dom_blocks[:, :, None] == jnp.arange(fit_blocks, dtype=jnp.int32)[None, None, :]
    ).astype(jnp.float32)
    local_density = jnp.einsum("isf,isr->fr", one_hot, pair_part.reshape(lmo_count, slots, block))
    density = lax.psum(local_density, ("occ", "ao"))
    density = density.reshape(fit_blocks * block)
    partial_value = jnp.einsum(
        "ipm,ipn->mn",
        fitted,
        lax.all_gather(fitted, "ao", axis=2, tiled=True),
        preferred_element_type=jnp.float32,
    )
    exchange_k = lax.psum_scatter(partial_value, "occ", scatter_dimension=1, tiled=True)
    return (exchange_k, density)


def solution(mesh):
    in_specs = (P("ao", "occ"), P("occ", None, "ao"), P(), P("occ", None), P("occ"))
    out_specs = (P("ao", "occ"), P())
    return jax.shard_map(
        on_device, mesh=mesh, in_specs=in_specs, out_specs=out_specs, check_vma=False
    )
```

profile of v0, /device:TPU:0, one launch (start us, length us, event | category | flops | bytes accessed | tf_op | source)
XLA Modules:
  0.0 159.3 jit_solution(12443113816982479165)
XLA Ops:
  7.2 0.0 copy-start
  7.2 0.0 all-gather.2.cloned.1.call-start
  8.0 0.7 fusion.5
  8.7 0.1 copy-done
  8.8 0.6 gather_fusion
  9.4 2.7 %select_convert_fusion = bf16[8,128,512]{2,1,0:T(8,128)(2,1)} fusion(bf16[8,128,128]{2,1,0:T(8,128)(2,1)S(1)} %gather_fusion, bf16[8,128,512]{2,1,0:T(8,128)(2,1)} %bitcast.25, pred[8]{0:T(512)(128)(4,1)S(1)} %iota_compare_fusion.2), kind=kOutput, calls=%fused_computation.3 | convolution fusion | flops 135266304 | bytes 2359304 | tf_op jit(solution)/shard_map/isab,isbm->isam/dot_general | solution.py:14
  12.1 0.0 all-gather.2.cloned.1.call-update
  12.1 0.0 reduce-scatter.2.cloned.1.call-start
  12.1 83.6 %all-gather.2.cloned.1.call-done = bf16[1,1024,2048]{2,1,0:T(8,128)(2,1)} async-done(((bf16[1,1024,512]{2,1,0:T(8,128)(2,1)}), bf16[1,1024,2048]{2,1,0:T(8,128)(2,1)}) %all-gather.2.cloned.1.call-update) | async-done | bytes 4194320 | tf_op jit(solution)/shard_map/all_gather | solution.py:30
  95.7 6.8 %fusion = f32[512,2048]{1,0:T(8,128)} fusion(bf16[1024,512]{1,0:T(8,128)(2,1)} %bitcast.24, bf16[1,1024,2048]{2,1,0:T(8,128)(2,1)} %all-gather.2.cloned.1.call-done), kind=kOutput, calls=%fused_computation.1 | convolution fusion | flops 2147483648 | bytes 9437184 | tf_op jit(solution)/shard_map/ipm,ipn->mn/dot_general | solution.py:27
  102.5 0.0 copy-start.1
  102.5 0.0 copy-start.2
  102.5 0.0 copy-start.3
  102.5 0.0 reduce-scatter.2.cloned.1.call-update
  102.6 1.2 copy-done.1
  103.8 0.0 copy-done.2
  103.8 0.4 fusion.2
  104.1 0.0 copy-done.3
  104.1 0.3 convolution_bitcast_fusion
  104.4 39.3 %psum.7 = f32[8192]{0:T(1024)} all-reduce(f32[8192]{0:T(1024)S(1)} %convolution_bitcast_fusion), channel_id=1, replica_groups=mesh['occ'=8,'ao'=4] {'occ','ao'}, use_global_device_ids=true, to_apply=%region_1.2 | all-reduce | flops 8192 | bytes 65536 | tf_op jit(solution)/shard_map/psum | solution.py:25
  143.7 8.8 %reduce-scatter.2.cloned.1.call-done = f32[512,256]{1,0:T(8,128)} async-done(((f32[512,2048]{1,0:T(8,128)}), f32[512,256]{1,0:T(8,128)}) %reduce-scatter.2.cloned.1.call-update) | async-done | bytes 524304 | tf_op jit(solution)/shard_map/reduce_scatter | solution.py:33
  (2 shorter events, 0.0 us)
Async XLA Ops:
  7.2 1.6 %copy-start = (bf16[64,128,128]{2,1,0:T(8,128)(2,1)S(1)}, bf16[64,128,128]{2,1,0:T(8,128)(2,1)}, u32[]{:S(2)}) copy-start(bf16[64,128,128]{2,1,0:T(8,128)(2,1)} %param.7) | copy-start | bytes 6291460
  7.2 88.5 %all-gather.2.cloned.1.call-start = ((), (), s32[]{:S(2)}) async-start(), calls=%async_computation.1 | async-start | bytes 5242880 | tf_op jit(solution)/shard_map/all_gather | solution.py:30
  12.1 140.4 %reduce-scatter.2.cloned.1.call-start = ((), (), s32[]{:S(2)}) async-start(), calls=%async_computation.2 | async-start | bytes 4718592 | tf_op jit(solution)/shard_map/reduce_scatter | solution.py:33
  102.5 1.2 copy-start.1
  102.5 1.2 copy-start.2
  102.5 1.6 copy-start.3
Sparse Core Ops, SparseCore 0:
  12.2 83.4 all-gather.1
  102.7 49.7 reduce-scatter.1
where the time goes:
time: 160 us; the launch traced here: 159 us
  waiting for transfers between devices  92.3 us (58%)
  blocking collectives  39.3 us (25%)
  between operations  14.8 us (9%)
  matrix products  10.2 us (6%)
  local copies, waits for them, and re-layouts  1.89 us (1%)
    all_gather x1, waiting for transfers between devices, on_device(): lax.all_gather(fitted, 'ao', axis=2, tiled=True)  83.6 us
    psum x1, blocking collectives, on_device(): density = lax.psum(local_density, ('occ', 'ao'))  39.3 us
    reduce_scatter x1, waiting for transfers between devices, on_device(): lax.psum_scatter(partial_value, 'occ', scatter_dimension=1, tiled=True)  8.75 us
    dot_general x1, matrix products, on_device(): jnp.einsum('ipm,ipn->mn', fitted, lax.all_gather(fitted, 'ao', axis=2, ti...  6.82 us
  transfers between devices with their start and end apart: 2, of which 2 were waited for; matrix products, arithmetic and copies ran while one was open for 0% of the time, Pallas kernels for 0%

commit v1 on v0

--- a/solution.py
+++ b/solution.py
@@ -2,6 +2,24 @@
 import jax.numpy as jnp
 from jax import lax
 from jax.sharding import PartitionSpec as P
+
+
+def work_around(x, axis, dim, apply, out_dim):
+    peers, position, rows = (lax.axis_size(axis), lax.axis_index(axis), x.shape[dim])
+    right = [(i, (i + 1) % peers) for i in range(peers)]
+    held, out = (x, None)
+    for lap in range(peers):
+        source = (position - lap) % peers
+        coming = lax.ppermute(held, axis, right) if lap < peers - 1 else None
+        made = apply(held, source * rows)
+        length = made.shape[out_dim]
+        if out is None:
+            out = jnp.zeros(
+                (*made.shape[:out_dim], peers * length, *made.shape[out_dim + 1 :]), made.dtype
+            )
+        out = lax.dynamic_update_slice_in_dim(out, made, source * length, axis=out_dim)
+        held = coming
+    return out
 
 
 def on_device(coef, half_ints, metric_inv, dom_blocks, dom_len):
@@ -24,11 +42,14 @@
     local_density = jnp.einsum("isf,isr->fr", one_hot, pair_part.reshape(lmo_count, slots, block))
     density = lax.psum(local_density, ("occ", "ao"))
     density = density.reshape(fit_blocks * block)
-    partial_value = jnp.einsum(
-        "ipm,ipn->mn",
+    partial_value = work_around(
         fitted,
-        lax.all_gather(fitted, "ao", axis=2, tiled=True),
-        preferred_element_type=jnp.float32,
+        "ao",
+        2,
+        lambda shard, start: jnp.einsum(
+            "ipm,ipn->mn", fitted, shard, preferred_element_type=jnp.float32
+        ),
+        1,
     )
     exchange_k = lax.psum_scatter(partial_value, "occ", scatter_dimension=1, tiled=True)
     return (exchange_k, density)

time: 160 us -> 152 us (0.950)
  waiting for transfers between devices: 92.3 us -> 78.2 us
  starting transfers between devices: 0.08 us -> 3.14 us
  local copies, waits for them, and re-layouts: 1.89 us -> 4.13 us
  matrix products: 10.2 us -> 11.9 us
    all_gather x1 -> x0, waiting for transfers between devices: 83.6 us -> none  [on_device(): lax.all_gather(fitted, 'ao', axis=2, tiled=True)]
    ppermute x0 -> x3, waiting for transfers between devices: none -> 67.9 us  [work_around(): coming = lax.ppermute(held, axis, right) if lap < peers - 1 else None]
    ppermute x0 -> x3, starting transfers between devices: none -> 3.11 us  [work_around(): coming = lax.ppermute(held, axis, right) if lap < peers - 1 else None]
    dot_general x1 -> x4, matrix products: 6.82 us -> 9.56 us  [on_device(): jnp.einsum('ipm,ipn->mn', fitted, shard, preferred_element_type=jnp.float32)]
    broadcast_in_dim x0 -> x1, local copies, waits for them, and re-layouts: none -> 2.45 us  [work_around(): jnp.zeros((*made.shape[:out_dim], peers * length, *made.shape[out_dim + 1...]
  transfers between devices with their start and end apart: 2 -> 4, of which waited for: 2 -> 4; matrix products, arithmetic and copies ran while one was open for 0% -> 6% of each run, Pallas kernels for 0% -> 0%
where the time goes in v1:
time: 152 us; the launch traced here: 151 us
  waiting for transfers between devices  78.2 us (51%)
  blocking collectives  38.3 us (25%)
  between operations  14.7 us (10%)
  matrix products  11.9 us (8%)
  local copies, waits for them, and re-layouts  4.13 us (3%)
  starting transfers between devices  3.14 us (2%)
    ppermute x3, waiting for transfers between devices, work_around(): coming = lax.ppermute(held, axis, right) if lap < peers - 1 else None  67.9 us
    psum x1, blocking collectives, on_device(): density = lax.psum(local_density, ('occ', 'ao'))  38.3 us
    reduce_scatter x1, waiting for transfers between devices, on_device(): lax.psum_scatter(partial_value, 'occ', scatter_dimension=1, tiled=True)  10.3 us
    dot_general x4, matrix products, on_device(): jnp.einsum('ipm,ipn->mn', fitted, shard, preferred_element_type=jnp.float32)  9.56 us
    ppermute x3, starting transfers between devices, work_around(): coming = lax.ppermute(held, axis, right) if lap < peers - 1 else None  3.11 us
  transfers between devices with their start and end apart: 4, of which 4 were waited for; matrix products, arithmetic and copies ran while one was open for 6% of the time, Pallas kernels for 0%

profile of v1, /device:TPU:0, one launch (start us, length us, event | category | flops | bytes accessed | tf_op | source)
XLA Modules:
  0.0 151.2 jit_solution(614908930677177998)
XLA Ops:
  7.2 0.0 copy-start
  7.2 0.0 reduce-scatter.2.cloned.1.call-start
  7.2 0.8 fusion.7
  8.7 0.1 copy-done
  8.8 0.6 gather_fusion
  9.4 1.6 %select_convert_fusion = bf16[8,128,512]{2,1,0:T(8,128)(2,1)S(1)} fusion(bf16[8,128,128]{2,1,0:T(8,128)(2,1)S(1)} %gather_fusion, bf16[8,128,512]{2,1,0:T(8,128)(2,1)} %bitcast.41, pred[8]{0:T(512)(128)(4,1)S(1)} %iota_compare_fusion.2), kind=kOutput, calls=%fused_computation.1 | convolution fusion | flops 135266304 | bytes 2359304 | tf_op jit(solution)/shard_map/isab,isbm->isam/dot_general | solution.py:32
  11.0 3.1 %collective-permute-start = (bf16[1,1024,512]{2,1,0:T(8,128)(2,1)S(1)}, bf16[1,1024,512]{2,1,0:T(8,128)(2,1)S(1)}, u32[]{:S(2)}, u32[]{:S(2)}) collective-permute-start(bf16[1,1024,512]{2,1,0:T(8,128)(2,1)S(1)} %bitcast.37), channel_id=1, source_target_pairs={{0,1},{1,2},{2,3},{3,0},{4,5},{5,6},{6,7},{7,4},{8,9},{9,10},{10,1... | collective-permute-start | bytes 3145736 | tf_op jit(solution)/shard_map/ppermute | solution.py:13
  14.1 25.2 %collective-permute-done = bf16[1,1024,512]{2,1,0:T(8,128)(2,1)S(1)} collective-permute-done((bf16[1,1024,512]{2,1,0:T(8,128)(2,1)S(1)}, bf16[1,1024,512]{2,1,0:T(8,128)(2,1)S(1)}, u32[]{:S(2)}, u32[]{:S(2)}) %collective-permute-start) | collective-permute-done | bytes 1048608 | tf_op jit(solution)/shard_map/ppermute | solution.py:13
  39.3 0.0 copy-start.2
  39.3 1.0 copy-done.2
  40.3 0.0 collective-permute-start.1
  40.3 26.2 %collective-permute-done.1 = bf16[1,1024,512]{2,1,0:T(8,128)(2,1)} collective-permute-done((bf16[1,1024,512]{2,1,0:T(8,128)(2,1)S(1)}, bf16[1,1024,512]{2,1,0:T(8,128)(2,1)}, u32[]{:S(2)}, u32[]{:S(2)}) %collective-permute-start.1) | collective-permute-done | bytes 1048608 | tf_op jit(solution)/shard_map/ppermute | solution.py:13
  66.5 0.0 collective-permute-start.2
  66.5 0.0 copy-start.3
  66.5 2.4 %broadcast_in_dim.23 = f32[512,2048]{1,0:T(8,128)} broadcast(f32[]{:T(128)} %constant.38.clone.1), dimensions={} | broadcast | bytes 4194308 | tf_op jit(solution)/shard_map/broadcast_in_dim | solution.py:17
  69.0 1.8 %fusion = f32[512,2048]{1,0:T(8,128)} fusion(f32[512,2048]{1,0:T(8,128)} %broadcast_in_dim.23, s32[]{:T(128)S(6)} %select_n.42, bf16[8,128,512]{2,1,0:T(8,128)(2,1)S(1)} %select_convert_fusion), kind=kOutput, calls=%fused_computation.6 | convolution fusion | flops 536870912 | bytes 3145732 | tf_op jit(solution)/shard_map/ipm,ipn->mn/dot_general | solution.py:49
  70.7 0.0 copy-done.3
  70.7 1.8 %convolution_dynamic-update-slice_fusion.2 = f32[512,2048]{1,0:T(8,128)} fusion(f32[512,2048]{1,0:T(8,128)} %fusion, s32[]{:T(128)S(6)} %select_n.44, bf16[1024,512]{1,0:T(8,128)(2,1)S(1)} %bitcast.38, bf16[1,1024,512]{2,1,0:T(8,128)(2,1)S(1)} %copy-done.3), kind=kOutput, calls=%fused_computation.4 | convolution fusion | flops 536870912 | bytes 3145732 | tf_op jit(solution)/shard_map/ipm,ipn->mn/dot_general | solution.py:49
  72.6 3.0 %convolution_dynamic-update-slice_fusion.1 = f32[512,2048]{1,0:T(8,128)} fusion(f32[512,2048]{1,0:T(8,128)} %convolution_dynamic-update-slice_fusion.2, s32[]{:T(128)S(6)} %select_n.46, bf16[1024,512]{1,0:T(8,128)(2,1)S(1)} %bitcast.39, bf16[1,1024,512]{2,1,0:T(8,128)(2,1)} %collective-permute-done.1), kind=kOutput, calls=%fused_computation.3 | convolution fusion | flops 536870912 | bytes 3145732 | tf_op jit(solution)/shard_map/ipm,ipn->mn/dot_general | solution.py:49
  75.6 0.0 copy-start.1
  75.6 0.0 copy-start.4
  75.6 16.5 %collective-permute-done.2 = bf16[1,1024,512]{2,1,0:T(8,128)(2,1)} collective-permute-done((bf16[1,1024,512]{2,1,0:T(8,128)(2,1)}, bf16[1,1024,512]{2,1,0:T(8,128)(2,1)}, u32[]{:S(2)}, u32[]{:S(2)}) %collective-permute-start.2) | collective-permute-done | bytes 1048608 | tf_op jit(solution)/shard_map/ppermute | solution.py:13
  92.1 3.0 %convolution_dynamic-update-slice_fusion = f32[512,2048]{1,0:T(8,128)} fusion(f32[512,2048]{1,0:T(8,128)} %convolution_dynamic-update-slice_fusion.1, s32[]{:T(128)S(6)} %select_n.48, bf16[1024,512]{1,0:T(8,128)(2,1)S(1)} %bitcast.40, bf16[1,1024,512]{2,1,0:T(8,128)(2,1)} %collective-permute-done.2), kind=kOutput, calls=%fused_computation.2 | convolution fusion | flops 536870912 | bytes 3145732 | tf_op jit(solution)/shard_map/ipm,ipn->mn/dot_general | solution.py:49
  95.1 0.0 reduce-scatter.2.cloned.1.call-update
  95.1 0.0 copy-done.1
  95.1 0.4 fusion.4
  95.5 0.0 copy-done.4
  95.5 0.3 convolution_bitcast_fusion.1
  95.7 38.3 %psum.7 = f32[8192]{0:T(1024)} all-reduce(f32[8192]{0:T(1024)S(1)} %convolution_bitcast_fusion.1), channel_id=1, replica_groups=mesh['occ'=8,'ao'=4] {'occ','ao'}, use_global_device_ids=true, to_apply=%region_1.2 | all-reduce | flops 8192 | bytes 65536 | tf_op jit(solution)/shard_map/psum | solution.py:43
  134.1 10.3 %reduce-scatter.2.cloned.1.call-done = f32[512,256]{1,0:T(8,128)} async-done(((f32[512,2048]{1,0:T(8,128)}), f32[512,256]{1,0:T(8,128)}) %reduce-scatter.2.cloned.1.call-update) | async-done | bytes 524304 | tf_op jit(solution)/shard_map/reduce_scatter | solution.py:54
  (2 shorter events, 0.0 us)
Async XLA Ops:
  7.2 1.6 %copy-start = (bf16[64,128,128]{2,1,0:T(8,128)(2,1)S(1)}, bf16[64,128,128]{2,1,0:T(8,128)(2,1)}, u32[]{:S(2)}) copy-start(bf16[64,128,128]{2,1,0:T(8,128)(2,1)} %param.7) | copy-start | bytes 6291460
  7.2 137.2 %reduce-scatter.2.cloned.1.call-start = ((), (), s32[]{:S(2)}) async-start(), calls=%async_computation.1 | async-start | bytes 4718592 | tf_op jit(solution)/shard_map/reduce_scatter | solution.py:54
  11.0 28.3 %collective-permute-start = (bf16[1,1024,512]{2,1,0:T(8,128)(2,1)S(1)}, bf16[1,1024,512]{2,1,0:T(8,128)(2,1)S(1)}, u32[]{:S(2)}, u32[]{:S(2)}) collective-permute-start(bf16[1,1024,512]{2,1,0:T(8,128)(2,1)S(1)} %bitcast.37), channel_id=1, source_target_pairs={{0,1},{1,2},{2,3},{3,0},{4,5},{5,6},{6,7},{7,4},{8,9},{9,10},{10,1... | collective-permute-start | bytes 3145736 | tf_op jit(solution)/shard_map/ppermute | solution.py:13
  39.3 1.0 copy-start.2
  40.3 26.2 %collective-permute-start.1 = (bf16[1,1024,512]{2,1,0:T(8,128)(2,1)S(1)}, bf16[1,1024,512]{2,1,0:T(8,128)(2,1)}, u32[]{:S(2)}, u32[]{:S(2)}) collective-permute-start(bf16[1,1024,512]{2,1,0:T(8,128)(2,1)S(1)} %collective-permute-done), channel_id=1, source_target_pairs={{0,1},{1,2},{2,3},{3,0},{4,5},{5,6},{6,7},{7,4},{8,9},{9,10},{10,1... | collective-permute-start | bytes 3145736 | tf_op jit(solution)/shard_map/ppermute | solution.py:13
  66.5 25.6 %collective-permute-start.2 = (bf16[1,1024,512]{2,1,0:T(8,128)(2,1)}, bf16[1,1024,512]{2,1,0:T(8,128)(2,1)}, u32[]{:S(2)}, u32[]{:S(2)}) collective-permute-start(bf16[1,1024,512]{2,1,0:T(8,128)(2,1)} %collective-permute-done.1), channel_id=1, source_target_pairs={{0,1},{1,2},{2,3},{3,0},{4,5},{5,6},{6,7},{7,4},{8,9},{9,10},{10,1... | collective-permute-start | bytes 3145736 | tf_op jit(solution)/shard_map/ppermute | solution.py:13
  66.5 4.2 %copy-start.3 = (bf16[1,1024,512]{2,1,0:T(8,128)(2,1)S(1)}, bf16[1,1024,512]{2,1,0:T(8,128)(2,1)}, u32[]{:S(2)}) copy-start(bf16[1,1024,512]{2,1,0:T(8,128)(2,1)} %copy-done.2) | copy-start | bytes 3145732
  75.6 19.5 %copy-start.1 = (bf16[512,1]{0,1:T(2,128)(2,1)S(1)}, bf16[512,1]{0,1:T(2,128)(2,1)}, u32[]{:S(2)}) copy-start(bf16[512,1]{0,1:T(2,128)(2,1)} %param.5) | copy-start | bytes 3076
  75.6 19.9 %copy-start.4 = (s32[1,8]{1,0:T(1,128)S(1)}, s32[1,8]{1,0:T(1,128)}, u32[]{:S(2)}) copy-start(s32[1,8]{1,0:T(1,128)} %param.8) | copy-start | bytes 100
Sparse Core Ops, SparseCore 0:
  95.2 49.0 reduce-scatter.1
